TPU v7x, 256 devices: a whole 4x4x8 slice. The times are simulated.
256 devices in a mesh: group: 8 (over z), tp: 32 (over y, x, core).
Axes of the slice: x: 4, y: 4, z: 8, core: 2. Of those that a mesh axis runs over, the one named last changes fastest.
Arguments:
- hidden_in: bfloat16 [512, 7168], P(('group', 'tp')), parts along dimension 0, may hold values from -4 to 4
- queries: bfloat16 [512, 32, 576], P(('group', 'tp')), parts along dimension 0, may hold values from -300 to 300
- cache: bfloat16 [512, 224, 576], P(('group', 'tp')), parts along dimension 0, may hold values from -4 to 4
- lengths: int32 [512], P(('group', 'tp')), parts along dimension 0, may hold values from 2 to 224, as said below
- w_uv: bfloat16 [32, 512, 128], P('tp'), may hold values from -0.5 to 0.5
- w_out: bfloat16 [4096, 7168], P('tp'), may hold values from -0.1875 to 0.1875
- norm_gain: bfloat16 [7168], replicated, may hold values from 0.5 to 1.5
- w_gate: bfloat16 [7168, 9216], P(None, 'tp'), may hold values from -0.0625 to 0.0625
- w_up: bfloat16 [7168, 9216], P(None, 'tp'), may hold values from -0.0625 to 0.0625
Outputs:
- attended: bfloat16 [512, 7168], P(('group', 'tp')), parts along dimension 0
- mlp_hidden: bfloat16 [512, 9216], P('group', 'tp'), parts along dimension 0
There are 8 independent parts, one for each index of `group`. A program takes and returns all parts, laid end to end along the dimension named above; an argument that names none is the same for every part. Nothing has to cross between parts.
Inputs may be any that keep to these rules, and one draw needn't show every extreme that they name: `lengths`: in every draw some request has exactly 224 valid positions.
All inputs are finite; a program needn't handle non-finite values.
Results may differ from a plain program's by a relative error of at most 0.017.
Values may be sent and summed in bfloat16 or wider, within the bound.
A program may use at most 64 MiB of HBM per device.

v0:
```python
import math

import jax
import jax.numpy as jnp
from jax import lax
from jax.sharding import PartitionSpec as P


def per_device(hidden_in, queries, cache, lengths, w_uv, w_out, norm_gain, w_gate, w_up):
    req_rows = queries.shape[0]
    heads_all = queries.shape[1]
    latent_dim = w_uv.shape[1]
    value_dim = w_uv.shape[2]
    rotary_dim = queries.shape[2] - latent_dim
    score_scale = 1.0 / math.sqrt(value_dim + rotary_dim)
    block_len = 32
    block_total = (jnp.max(lengths) + block_len - 1) // block_len

    def block_scores(block_index):
        piece = lax.dynamic_slice_in_dim(cache, block_index * block_len, block_len, 1)
        scores = (
            jnp.einsum("rhk,rjk->rhj", queries, piece, preferred_element_type=jnp.float32)
            * score_scale
        )
        position = block_index * block_len + lax.iota(jnp.int32, block_len)
        visible = position[None, None, :] < lengths[:, None, None]
        return (piece, scores, visible)

    def find_max(block_index, row_max):
        piece, scores, visible = block_scores(block_index)
        return jnp.maximum(row_max, jnp.max(jnp.where(visible, scores, -1e30), axis=-1))

    row_max = lax.fori_loop(
        0, block_total, find_max, jnp.full((req_rows, heads_all), -1e30, jnp.float32)
    )

    def accumulate(block_index, carry):
        summed, weight_total = carry
        piece, scores, visible = block_scores(block_index)
        probs_full = jnp.exp(jnp.where(visible, scores - row_max[:, :, None], -1e30))
        probs_low = probs_full.astype(jnp.bfloat16)
        summed = summed + jnp.einsum(
            "rhj,rjl->rhl", probs_low, piece[:, :, :latent_dim], preferred_element_type=jnp.float32
        )
        return (summed, weight_total + jnp.sum(probs_full, axis=-1))

    start_carry = (
        jnp.zeros((req_rows, heads_all, latent_dim), jnp.float32),
        jnp.zeros((req_rows, heads_all), jnp.float32),
    )
    summed, weight_total = lax.fori_loop(0, block_total, accumulate, start_carry)
    context = (summed / weight_total[:, :, None]).astype(jnp.bfloat16)
    head_context = lax.all_to_all(context, "tp", split_axis=1, concat_axis=0, tiled=True)
    values = jnp.einsum(
        "thl,hlv->thv", head_context, w_uv, preferred_element_type=jnp.float32
    ).astype(jnp.bfloat16)
    values = values.reshape(values.shape[0], values.shape[1] * values.shape[2])
    row_offset = lax.axis_index("tp") * req_rows
    partial_out = jnp.dot(values, w_out, preferred_element_type=jnp.float32)
    own_rows = lax.dynamic_slice_in_dim(partial_out, row_offset, req_rows, 0) + hidden_in.astype(
        jnp.float32
    )
    partial_out = lax.dynamic_update_slice_in_dim(partial_out, own_rows, row_offset, 0)
    residual_all = lax.psum(partial_out, "tp")
    residual = lax.dynamic_slice_in_dim(residual_all, row_offset, req_rows, 0)
    attended = residual.astype(jnp.bfloat16)
    mean_square = jnp.mean(residual_all * residual_all, axis=-1, keepdims=True)
    normed_rows = (
        residual_all * lax.rsqrt(mean_square + 1e-06) * norm_gain.astype(jnp.float32)
    ).astype(jnp.bfloat16)
    gate_part = jnp.dot(normed_rows, w_gate, preferred_element_type=jnp.float32)
    up_part = jnp.dot(normed_rows, w_up, preferred_element_type=jnp.float32)
    mlp_hidden = (jax.nn.silu(gate_part) * up_part).astype(jnp.bfloat16)
    return (attended, mlp_hidden)


def solution(mesh):
    in_specs = (
        P(("group", "tp"), None),
        P(("group", "tp"), None, None),
        P(("group", "tp"), None, None),
        P(("group", "tp")),
        P("tp", None, None),
        P("tp", None),
        P(),
        P(None, "tp"),
        P(None, "tp"),
    )
    out_specs = (P(("group", "tp"), None), P("group", "tp"))
    return jax.shard_map(
        per_device, mesh=mesh, in_specs=in_specs, out_specs=out_specs, check_vma=False
    )
```

profile of v0, /device:TPU:1, one launch (start us, length us, event | category | flops | bytes accessed | tf_op | source)
XLA Modules:
  0.0 193.1 jit_solution(17754625080127269544)
XLA Ops:
  7.2 0.0 copy-start
  7.2 1.4 reduce_max.18
  9.3 7.5 %while.22 = (s32[]{:T(128)}, f32[2,32]{1,0:T(2,128)S(1)}, s32[]{:T(128)}, s32[2]{0:T(128)}, bf16[2,224,576]{2,1,0:T(8,128)(2,1)}, /*index=5*/bf16[2,32,576]{2,1,...) while((s32[]{:T(128)}, f32[2,32]{1,0:T(2,128)S(1)}, s32[]{:T(128)}, s32[2]{0:T(128)}, ...), condition=%wide.region_3.4_spmd, body=%wide.region_1.3_spmd.sunk | while | flops 2365542 | bytes 165411 | solution.py:33
  9.3 0.7 broadcast_compare_fusion.4
  10.1 1.1 fusion.35
  11.2 0.7 broadcast_compare_fusion.4
  11.9 1.1 fusion.35
  13.1 0.7 broadcast_compare_fusion.4
  13.8 1.1 fusion.35
  14.9 0.7 broadcast_compare_fusion.4
  15.7 1.1 fusion.35
  16.8 0.0 copy-start.3
  16.8 11.9 %while.23 = (s32[]{:T(128)}, f32[2,32,512]{2,1,0:T(8,128)S(1)}, f32[2,32]{1,0:T(2,128)S(1)}, s32[]{:T(128)}, s32[2]{0:T(128)}, /*index=5*/bf16[2,224,576]{2,1,0:...) while((s32[]{:T(128)}, f32[2,32,512]{2,1,0:T(8,128)S(1)}, ...), condition=%wide.region_6.7_spmd, body=%wide.region_4.6_spmd.sunk | while | flops 4499558 | bytes 501559 | solution.py:51
  16.9 0.8 broadcast_compare_fusion.5
  17.6 1.1 fusion.39
  18.7 1.1 convolution_add_fusion.2
  19.9 0.7 broadcast_compare_fusion.5
  20.6 1.1 fusion.39
  21.7 1.1 convolution_add_fusion.2
  22.8 0.7 broadcast_compare_fusion.5
  23.5 1.1 fusion.39
  24.7 1.1 convolution_add_fusion.2
  25.8 0.7 broadcast_compare_fusion.5
  26.5 1.1 fusion.39
  27.6 1.1 convolution_add_fusion.2
  28.7 0.1 divide_convert_fusion
  28.8 0.7 copy.18
  29.5 19.4 %all-to-all-start = ((bf16[2,32,512]{2,0,1:T(2,128)(2,1)}), bf16[2,32,512]{2,0,1:T(2,128)(2,1)S(1)}, u32[]{:S(2)}, u32[]{:S(2)}) async-start(bf16[2,32,512]{2,0,1:T(2,128)(2,1)} %copy.18), calls=%async_computation | async-start | bytes 131072 | tf_op jit(solution)/shard_map/all_to_all | solution.py:53
  48.8 0.0 all-reduce.2.cloned.1.call-start
  48.9 7.3 %all-to-all-done = bf16[2,32,512]{2,0,1:T(2,128)(2,1)S(1)} async-done(((bf16[2,32,512]{2,0,1:T(2,128)(2,1)}), bf16[2,32,512]{2,0,1:T(2,128)(2,1)S(1)}, u32[]{:S(2)}, u32[]{:S(2)}) %all-to-all-start) | async-done | bytes 65568 | tf_op jit(solution)/shard_map/all_to_all | solution.py:53
  56.2 0.0 copy-done
  56.2 0.0 copy-done.3
  56.2 0.0 copy-start.4
  56.2 1.8 fusion.14
  58.0 0.0 copy-done.4
  58.0 0.0 copy-start.5
  58.0 1.6 add_dynamic-update-slice_fusion
  59.6 0.0 all-reduce.2.cloned.1.call-update
  59.7 0.0 copy-done.5
  59.7 118.0 %all-reduce.2.cloned.1.call-done = f32[64,7168]{1,0:T(8,128)} async-done(((f32[64,7168]{1,0:T(8,128)}), f32[64,7168]{1,0:T(8,128)}) %all-reduce.2.cloned.1.call-update) | async-done | bytes 1835024 | tf_op jit(solution)/shard_map/psum | solution.py:64
  177.6 0.0 copy-start.1
  177.6 1.9 multiply_reduce_fusion
  179.5 0.2 copy-done.1
  179.7 0.6 dynamic-slice_convert_fusion
  180.3 0.0 copy-start.2
  180.3 3.8 %fusion.17 = f32[64,288]{1,0:T(8,128)S(1)} fusion(bf16[7168,288]{0,1:T(8,128)(2,1)} %param.20, f32[64,7168]{1,0:T(8,128)S(1)} %copy-done.1, f32[7168]{0:T(1024)S(1)} %convert_element_type.31, f32[64]{0:T(128)S(1)} %add_rsqrt_fusion), kind=kOutput, calls=%fused_computation.31 | convolution fusion | flops 265617408 | bytes 6066432 | tf_op jit(solution)/shard_map/dot_general | solution.py:71
  184.1 0.0 copy-done.2
  184.2 2.1 %fusion.13 = bf16[64,288]{1,0:T(8,128)(2,1)} fusion(bf16[7168,288]{0,1:T(8,128)(2,1)S(1)} %copy-done.2, f32[64,288]{1,0:T(8,128)S(1)} %fusion.17, f32[64,7168]{1,0:T(8,128)S(1)} %copy-done.1, f32[7168]{0:T(1024)S(1)} %convert_element_type.31, f32[64]{0:T(128)S(1)} %add_rsqrt_fusion), kind=kOutput, calls=%fused_computation.23 | convolution fusion | flops 265728000 | bytes 6103296 | tf_op jit(solution)/shard_map/dot_general | solution.py:72
  (22 shorter events, 0.2 us)
Async XLA Ops:
  7.2 49.0 %copy-start = (bf16[128,7168]{1,0:T(8,128)(2,1)S(1)}, bf16[128,7168]{1,0:T(8,128)(2,1)}, u32[]{:S(2)}) copy-start(bf16[128,7168]{1,0:T(8,128)(2,1)} %param.18) | copy-start | bytes 5505028
  16.8 39.4 %copy-start.3 = (bf16[1,512,128]{2,1,0:T(8,128)(2,1)S(1)}, bf16[1,512,128]{2,1,0:T(8,128)(2,1)}, u32[]{:S(2)}) copy-start(bf16[1,512,128]{2,1,0:T(8,128)(2,1)} %param.17) | copy-start | bytes 393220
  29.5 26.7 %all-to-all-start = ((bf16[2,32,512]{2,0,1:T(2,128)(2,1)}), bf16[2,32,512]{2,0,1:T(2,128)(2,1)S(1)}, u32[]{:S(2)}, u32[]{:S(2)}) async-start(bf16[2,32,512]{2,0,1:T(2,128)(2,1)} %copy.18), calls=%async_computation | async-start | bytes 131072 | tf_op jit(solution)/shard_map/all_to_all | solution.py:53
  48.8 128.8 %all-reduce.2.cloned.1.call-start = ((), (), s32[]{:S(2)}) async-start(), calls=%async_computation.1 | async-start | bytes 3670016 | tf_op jit(solution)/shard_map/psum | solution.py:64
  56.2 1.8 copy-start.4
  58.0 1.7 copy-start.5
  177.6 2.1 %copy-start.1 = (f32[64,7168]{1,0:T(8,128)S(1)}, f32[64,7168]{1,0:T(8,128)}, u32[]{:S(2)}) copy-start(f32[64,7168]{1,0:T(8,128)} %all-reduce.2.cloned.1.call-done) | copy-start | bytes 5505028
  180.3 3.8 %copy-start.2 = (bf16[7168,288]{0,1:T(8,128)(2,1)S(1)}, bf16[7168,288]{0,1:T(8,128)(2,1)}, u32[]{:S(2)}) copy-start(bf16[7168,288]{0,1:T(8,128)(2,1)} %param.21) | copy-start | bytes 12386308
Sparse Core Ops, SparseCore 0:
  59.8 117.8 all-reduce.1
where the time goes:
time: 194 us; the launch traced here: 193 us
  waiting for transfers between devices  125 us (64%)
  matrix products  20.8 us (11%)
  starting transfers between devices  19.4 us (10%)
  between operations  14.8 us (8%)
  other arithmetic  11 us (6%)
    psum x1, waiting for transfers between devices, per_device(): residual_all = lax.psum(partial_out, 'tp')  118 us
    all_to_all x1, starting transfers between devices, per_device(): lax.all_to_all(context, 'tp', split_axis=1, concat_axis=0, tiled=True)  19.4 us
    dot_general x8, matrix products, block_scores(): jnp.einsum('rhk,rjk->rhj', queries, piece, preferred_element_type=jnp.flo...  8.8 us
    all_to_all x1, waiting for transfers between devices, per_device(): lax.all_to_all(context, 'tp', split_axis=1, concat_axis=0, tiled=True)  7.27 us
    lt x8, other arithmetic, block_scores(): visible = position[None, None, :] < lengths[:, None, None]  5.87 us
    dot_general x4, matrix products, accumulate(): jnp.einsum('rhj,rjl->rhl', probs_low, piece[:, :, :latent_dim], preferred...  4.26 us
  transfers between devices with their start and end apart: 2, of which 2 were waited for; matrix products, arithmetic and copies ran while one was open for 0% of the time, Pallas kernels for 0%

commit v1 on v0

v1 whole, which is shorter than its diff:
```python
import math

import jax
import jax.numpy as jnp
from jax import lax
from jax.experimental import pallas as pl
from jax.experimental.pallas import tpu as pltpu
from jax.sharding import PartitionSpec as P

MESH = pl.DeviceIdType.MESH
SIDE = 4
CHIPS = SIDE * SIDE
LANES = 128
OFFSETS = sorted(
    ((dx, dy) for dx in range(SIDE) for dy in range(SIDE)),
    key=lambda o: -(min(o[0], SIDE - o[0]) + min(o[1], SIDE - o[1])),
)
COLUMN_ORDER = (2, 1, 3, 0)


def make_kernel(req, heads, latent, value, rotary, width, hidden, positions):
    tokens = req * 2 * CHIPS
    half = width // 2
    block = half // SIDE
    rows = tokens // SIDE
    score_scale = 1.0 / math.sqrt(value + rotary)
    pieces = latent // LANES

    def kernel(
        lengths_ref, hid_hbm, q_hbm, cache_hbm, wuv_hbm, wout_hbm, gain_ref, wg_hbm, wu_hbm,
        att_ref, mlp_ref,
        q_v, cache_v, wuv_v, w2_v, hid_v, wg_v, wu_v, send_perm, recv_perm,
        ctx_send, ctx_recv, part_v, red_v, x_v,
        in_sem, w2_sem, hid_sem, w2x_send, w2x_recv, hidx_send, hidx_recv, wuvx_send, wuvx_recv,
        ctx_ssem, ctx_rsem, red_ssem, red_rsem, all_ssem, all_rsem, fwd_ssem, fwd_rsem,
    ):
        group = lax.axis_index("group")
        me = lax.axis_index("tp")
        core = lax.rem(me, 2)
        other = 1 - core
        chip = me // 2
        cx = lax.rem(chip, SIDE)
        cy = chip // SIDE

        def chip_at(dx, dy):
            return lax.rem(cy + dy, SIDE) * SIDE + lax.rem(cx + dx, SIDE)

        def remote(src, dst, ssem, rsem, target):
            return pltpu.make_async_remote_copy(
                src_ref=src, dst_ref=dst, send_sem=ssem, recv_sem=rsem,
                device_id=(group, target), device_id_type=MESH,
            )

        partner = chip * 2 + other

        load_cache = pltpu.make_async_copy(cache_hbm, cache_v, in_sem.at[0])
        load_q = pltpu.make_async_copy(q_hbm, q_v, in_sem.at[1])
        load_cache.start()
        load_q.start()
        barrier = pltpu.get_barrier_semaphore()
        for dx, dy in OFFSETS:
            for dc in range(2):
                if (dx, dy, dc) != (0, 0, 0):
                    target = chip_at(dx, dy) * 2 + lax.rem(core + dc, 2)
                    pl.semaphore_signal(
                        barrier, inc=1, device_id=(group, target), device_id_type=MESH
                    )
        load_wuv = pltpu.make_async_copy(wuv_hbm.at[0], wuv_v.at[core], in_sem.at[2])
        load_wuv.start()

        def columns(which, b):
            return pl.ds(pl.multiple_of(which * half + b * block, LANES), block)

        loads_w2 = []
        loads_hid = []
        for b in range(SIDE):
            loads_w2.append(
                pltpu.make_async_copy(
                    wout_hbm.at[:, columns(core, b)], w2_v.at[b, core], w2_sem.at[b]
                )
            )
            loads_hid.append(
                pltpu.make_async_copy(
                    hid_hbm.at[:, columns(core, b)], hid_v.at[b, core], hid_sem.at[b]
                )
            )
        for copy in loads_w2 + loads_hid:
            copy.start()
        load_wg = pltpu.make_async_copy(wg_hbm, wg_v, in_sem.at[3])
        load_wu = pltpu.make_async_copy(wu_hbm, wu_v, in_sem.at[4])
        load_wg.start()
        load_wu.start()

        size = CHIPS * 16
        row = lax.broadcasted_iota(jnp.int32, (size, size), 0)
        col = lax.broadcasted_iota(jnp.int32, (size, size), 1)
        to = row // 16
        item = row % 16
        src_row = ((item % 2) * pieces + (item // 2) % pieces) * heads + to * 2 + item // (2 * pieces)
        send_perm[...] = (col == src_row).astype(jnp.bfloat16)
        tok = row % 32
        src_row = (tok // 2) * 16 + (row // 32) * 2 + tok % 2
        recv_perm[...] = (col == src_row).astype(jnp.bfloat16)

        load_cache.wait()
        load_q.wait()
        position = lax.broadcasted_iota(jnp.int32, (heads, positions), 1)
        parts = []
        for r in range(req):
            keys = cache_v[r]
            scores = (
                lax.dot_general(
                    q_v[r], keys, (((1,), (1,)), ((), ())), preferred_element_type=jnp.float32
                )
                * score_scale
            )
            visible = position < lengths_ref[r]
            top = jnp.max(jnp.where(visible, scores, -1e30), axis=-1, keepdims=True)
            probs = jnp.exp(jnp.where(visible, scores - top, -1e30))
            total = jnp.sum(probs, axis=-1, keepdims=True)
            summed = jnp.dot(
                probs.astype(jnp.bfloat16), keys[:, :latent], preferred_element_type=jnp.float32
            )
            ctx = (summed / total).astype(jnp.bfloat16)
            for p in range(pieces):
                parts.append(ctx[:, p * LANES : (p + 1) * LANES])
        ctx_send[...] = (
            jnp.dot(
                send_perm[...], jnp.concatenate(parts, axis=0), preferred_element_type=jnp.float32
            )
            .astype(jnp.bfloat16)
            .reshape(CHIPS, 16, LANES)
        )

        pl.semaphore_wait(barrier, 2 * CHIPS - 1)

        sends = []
        for dx, dy in OFFSETS:
            for dc in range(2):
                if (dx, dy, dc) != (0, 0, 0):
                    to_chip = chip_at(dx, dy)
                    target = to_chip * 2 + lax.rem(core + dc, 2)
                    copy = remote(
                        ctx_send.at[to_chip], ctx_recv.at[me],
                        ctx_ssem.at[target], ctx_rsem.at[me], target,
                    )
                    copy.start()
                    sends.append(copy)
        trade_wuv = remote(
            wuv_hbm.at[0], wuv_v.at[core], wuvx_send.at[0], wuvx_recv.at[0], partner
        )
        trade_wuv.start()
        trade_w2 = []
        trade_hid = []
        for b in range(SIDE):
            trade_w2.append(
                remote(
                    wout_hbm.at[:, columns(other, b)], w2_v.at[b, core],
                    w2x_send.at[b], w2x_recv.at[b], partner,
                )
            )
            trade_hid.append(
                remote(
                    hid_hbm.at[:, columns(other, b)], hid_v.at[b, core],
                    hidx_send.at[b], hidx_recv.at[b], partner,
                )
            )
        for copy in trade_w2 + trade_hid:
            copy.start()
        ctx_recv[me] = ctx_send[chip]

        for copy in [load_wuv] + loads_w2 + loads_hid:
            copy.wait()
        trade_wuv.wait_recv()
        for copy in trade_w2 + trade_hid:
            copy.wait_recv()
        for dx, dy in reversed(OFFSETS):
            for dc in range(2):
                if (dx, dy, dc) != (0, 0, 0):
                    source = chip_at(dx, dy) * 2 + lax.rem(core + dc, 2)
                    remote(
                        ctx_send.at[0], ctx_recv.at[source],
                        ctx_ssem.at[source], ctx_rsem.at[source], source,
                    ).wait_recv()

        got = ctx_recv[...].reshape(2, size, LANES)
        ordered = [
            jnp.dot(recv_perm[...], got[k], preferred_element_type=jnp.float32).astype(jnp.bfloat16)
            for k in range(2)
        ]
        vals = []
        for h in range(2):
            ctx = jnp.concatenate(
                [
                    jnp.concatenate(
                        [o[(h * pieces + p) * 32 : (h * pieces + p + 1) * 32] for p in range(pieces)],
                        axis=1,
                    )
                    for o in ordered
                ],
                axis=0,
            )
            vals.append(
                jnp.dot(ctx, wuv_v[h], preferred_element_type=jnp.float32).astype(jnp.bfloat16)
            )
        vals = jnp.concatenate(vals, axis=1)

        token = lax.broadcasted_iota(jnp.int32, (tokens, block), 0)
        for dx in COLUMN_ORDER:
            b = lax.rem(cx + dx, SIDE)
            part = jnp.dot(
                vals, w2_v[b].reshape(2 * value, block), preferred_element_type=jnp.float32
            )
            own = hid_v[b].astype(jnp.float32)
            for h in range(2):
                for r in range(req):
                    part = part + jnp.where(
                        token == chip * (2 * req) + h * req + r, own[h, r : r + 1, :], 0.0
                    )
            part_v[b] = part.astype(jnp.bfloat16).reshape(SIDE, rows, block)
            for dy in COLUMN_ORDER:
                if (dx, dy) != (0, 0):
                    to_chip = chip_at(dx, dy)
                    copy = remote(
                        part_v.at[b, lax.rem(cy + dy, SIDE)], red_v.at[chip],
                        red_ssem.at[to_chip], red_rsem.at[chip], to_chip * 2 + core,
                    )
                    copy.start()
                    sends.append(copy)
        red_v[chip] = part_v[cx, cy]
        for dx, dy in reversed(OFFSETS):
            if (dx, dy) != (0, 0):
                source = chip_at(dx, dy)
                remote(
                    part_v.at[0, 0], red_v.at[source],
                    red_ssem.at[source], red_rsem.at[source], source * 2 + core,
                ).wait_recv()
        total = red_v[0].astype(jnp.float32)
        for k in range(1, CHIPS):
            total = total + red_v[k].astype(jnp.float32)
        x_v[core, cx, cy] = total.astype(jnp.bfloat16)

        for dx, dy in OFFSETS:
            if (dx, dy) != (0, 0):
                to_chip = chip_at(dx, dy)
                copy = remote(
                    x_v.at[core, cx, cy], x_v.at[core, cx, cy],
                    all_ssem.at[to_chip], all_rsem.at[chip], to_chip * 2 + core,
                )
                copy.start()
                sends.append(copy)

        load_wg.wait()
        load_wu.wait()
        gate = jnp.zeros((tokens, hidden), jnp.float32)
        up = jnp.zeros((tokens, hidden), jnp.float32)
        square = jnp.zeros((tokens, 1), jnp.float32)

        def multiply(which, b, carry):
            gate, up, square = carry
            x = x_v[which, b].reshape(tokens, block).astype(jnp.float32)
            square = square + jnp.sum(x * x, axis=-1, keepdims=True)
            x = (x * gain_ref[which * SIDE + b].astype(jnp.float32)).astype(jnp.bfloat16)
            span = pl.ds(pl.multiple_of(which * half + b * block, block), block)
            gate = gate + jnp.dot(x, wg_v[span, :], preferred_element_type=jnp.float32)
            up = up + jnp.dot(x, wu_v[span, :], preferred_element_type=jnp.float32)
            return (gate, up, square)

        carry = (gate, up, square)
        forwards = []
        for dx in reversed(COLUMN_ORDER):
            b = lax.rem(cx + dx, SIDE)
            for dy in reversed(COLUMN_ORDER):
                if (dx, dy) != (0, 0):
                    source = chip_at(dx, dy)
                    a = lax.rem(cy + dy, SIDE)
                    remote(
                        x_v.at[core, b, a], x_v.at[core, b, a],
                        all_ssem.at[source], all_rsem.at[source], source * 2 + core,
                    ).wait_recv()
            copy = remote(
                x_v.at[core, b], x_v.at[core, b], fwd_ssem.at[b], fwd_rsem.at[b], partner
            )
            copy.start()
            sends.append(copy)
            carry = multiply(core, b, carry)
        for dx in reversed(COLUMN_ORDER):
            b = lax.rem(cx + dx, SIDE)
            remote(
                x_v.at[other, b], x_v.at[other, b], fwd_ssem.at[b], fwd_rsem.at[b], partner
            ).wait_recv()
            carry = multiply(other, b, carry)
        gate, up, square = carry
        scale = lax.rsqrt(square / width + 1e-6)
        gate = gate * scale
        up = up * scale
        mlp_ref[...] = (gate / (1.0 + jnp.exp(-gate)) * up).astype(jnp.bfloat16)

        first = lax.rem(chip, SIDE) * (2 * req) + core * req
        line = lax.broadcasted_iota(jnp.int32, (rows, block), 0)
        for which in range(2):
            for b in range(SIDE):
                x = x_v[which, b, cy].astype(jnp.float32)
                picked = jnp.concatenate(
                    [
                        jnp.sum(jnp.where(line == first + r, x, 0.0), axis=0, keepdims=True)
                        for r in range(req)
                    ],
                    axis=0,
                )
                at = which * half + b * block
                att_ref[:, at : at + block] = picked.astype(jnp.bfloat16)

        for copy in sends + [trade_wuv] + trade_w2 + trade_hid:
            copy.wait_send()

    return kernel


def per_device(hidden_in, queries, cache, lengths, w_uv, w_out, norm_gain, w_gate, w_up):
    req, heads, depth = queries.shape
    positions = cache.shape[1]
    latent, value = w_uv.shape[1:]
    width, hidden = w_gate.shape
    rotary = depth - latent
    tokens = req * 2 * CHIPS
    half = width // 2
    block = half // SIDE
    rows = tokens // SIDE
    size = CHIPS * 16
    bf16 = jnp.bfloat16
    dma = pltpu.SemaphoreType.DMA
    hbm = pl.BlockSpec(memory_space=pl.ANY)
    vmem = pl.BlockSpec(memory_space=pltpu.VMEM)
    return pl.pallas_call(
        make_kernel(req, heads, latent, value, rotary, width, hidden, positions),
        out_shape=(
            jax.ShapeDtypeStruct((req, width), bf16),
            jax.ShapeDtypeStruct((tokens, hidden), bf16),
        ),
        in_specs=[pl.BlockSpec(memory_space=pltpu.SMEM), hbm, hbm, hbm, hbm, hbm, vmem, hbm, hbm],
        out_specs=(vmem, vmem),
        scratch_shapes=[
            pltpu.VMEM((req, heads, depth), bf16),
            pltpu.VMEM((req, positions, depth), bf16),
            pltpu.VMEM((2, latent, value), bf16),
            pltpu.VMEM((SIDE, 2, value, block), bf16),
            pltpu.VMEM((SIDE, 2, req, block), bf16),
            pltpu.VMEM((width, hidden), bf16),
            pltpu.VMEM((width, hidden), bf16),
            pltpu.VMEM((size, size), bf16),
            pltpu.VMEM((size, size), bf16),
            pltpu.VMEM((CHIPS, 16, LANES), bf16),
            pltpu.VMEM((2 * CHIPS, 16, LANES), bf16),
            pltpu.VMEM((SIDE, SIDE, rows, block), bf16),
            pltpu.VMEM((CHIPS, rows, block), bf16),
            pltpu.VMEM((2, SIDE, SIDE, rows, block), bf16),
            dma((5,)),
            dma((SIDE,)),
            dma((SIDE,)),
            dma((SIDE,)),
            dma((SIDE,)),
            dma((SIDE,)),
            dma((SIDE,)),
            dma((1,)),
            dma((1,)),
            dma((2 * CHIPS,)),
            dma((2 * CHIPS,)),
            dma((CHIPS,)),
            dma((CHIPS,)),
            dma((CHIPS,)),
            dma((CHIPS,)),
            dma((SIDE,)),
            dma((SIDE,)),
        ],
        compiler_params=pltpu.CompilerParams(
            collective_id=0, has_side_effects=True, vmem_limit_bytes=40 * 1024 * 1024
        ),
    )(
        lengths, hidden_in, queries, cache, w_uv, w_out,
        norm_gain.reshape(2 * SIDE, 1, block), w_gate, w_up,
    )


def solution(mesh):
    in_specs = (
        P(("group", "tp"), None),
        P(("group", "tp"), None, None),
        P(("group", "tp"), None, None),
        P(("group", "tp")),
        P("tp", None, None),
        P("tp", None),
        P(),
        P(None, "tp"),
        P(None, "tp"),
    )
    out_specs = (P(("group", "tp"), None), P("group", "tp"))
    return jax.shard_map(
        per_device, mesh=mesh, in_specs=in_specs, out_specs=out_specs, check_vma=False
    )
```

time: 194 us -> 55.7 us (0.29)
  waiting for transfers between devices: 125 us -> 0 us
  Pallas kernels: 0 us -> 32.5 us
  matrix products: 20.8 us -> 0 us
  local copies, waits for them, and re-layouts: 1.58 us -> 22 us
  starting transfers between devices: 19.4 us -> 0 us
  between operations: 14.8 us -> 0.7 us
  other arithmetic: 11 us -> 0 us
    psum x1 -> x0, waiting for transfers between devices: 118 us -> none  [per_device(): residual_all = lax.psum(partial_out, 'tp')]
    pallas_call x0 -> x1, Pallas kernels: none -> 32.5 us  [per_device(): pl.pallas_call(make_kernel(req, heads, latent, value, rotary, width, hidd...]
    unnamed x12 -> x20, local copies, waits for them, and re-layouts: 0.21 us -> 21.3 us
    dot_general x15 -> x0, matrix products: 20.8 us -> none  [the longest x8 8.8 us: block_scores(): jnp.einsum('rhk,rjk->rhj', queries, piece, preferred_element_type=jnp.flo...]
    all_to_all x1 -> x0, starting transfers between devices: 19.4 us -> none  [per_device(): lax.all_to_all(context, 'tp', split_axis=1, concat_axis=0, tiled=True)]
    all_to_all x1 -> x0, waiting for transfers between devices: 7.27 us -> none  [per_device(): lax.all_to_all(context, 'tp', split_axis=1, concat_axis=0, tiled=True)]
    lt x8 -> x0, other arithmetic: 5.87 us -> none  [block_scores(): visible = position[None, None, :] < lengths[:, None, None]]
  transfers between devices with their start and end apart: 2 -> 0, of which waited for: 2 -> 0; matrix products, arithmetic and copies ran while one was open for 0% -> 0% of each run, Pallas kernels for 0% -> 0%
where the time goes in v1:
time: 55.7 us; the launch traced here: 55.2 us
  Pallas kernels  32.5 us (58%)
  local copies, waits for them, and re-layouts  22 us (39%)
  between operations  0.7 us (1%)
    pallas_call x1, Pallas kernels, per_device(): pl.pallas_call(make_kernel(req, heads, latent, value, rotary, width, hidd...  32.5 us
    unnamed x20, local copies, waits for them, and re-layouts  21.3 us

profile of v1, /device:TPU:1, one launch (start us, length us, event | category | flops | bytes accessed | tf_op | source)
XLA Modules:
  0.0 55.2 jit_solution(842531479824229652)
XLA Ops:
  0.6 0.7 %reshape.8.gain_ref = bf16[8,1,896]{2,1,0:T(2,128)(2,1)S(1)} reshape(bf16[7168]{0:T(1024)(128)(2,1)} %param.15) | data formatting | bytes 28672 | tf_op jit(solution)/shard_map/reshape | solution.py:381
  1.4 7.4 %copy.14.wg_hbm = bf16[7168,288]{1,0:T(8,128)(2,1)} copy(bf16[7168,288]{0,1:T(8,128)(2,1)} %param.16) | data formatting | bytes 8257536 | tf_op args[7]
  8.7 0.0 copy-start.2
  8.7 0.0 copy-start.3
  8.7 0.0 copy-start.4
  8.7 0.0 copy-start.5
  8.8 0.0 copy-start.6
  8.8 0.0 copy-start.7
  8.8 7.5 %copy.15.wu_hbm = bf16[7168,288]{1,0:T(8,128)(2,1)} copy(bf16[7168,288]{0,1:T(8,128)(2,1)} %param.17) | data formatting | bytes 8257536 | tf_op args[8]
  16.3 0.0 copy-done.2
  16.3 0.0 copy-done.3
  16.3 0.0 copy-done.4
  16.3 0.0 copy-done.5
  16.3 0.0 copy-done.6
  16.3 0.0 copy-done.7
  16.3 0.0 copy-start
  16.4 2.6 %copy-done = bf16[7168,288]{1,0:T(8,128)(2,1)S(1)} copy-done((bf16[7168,288]{1,0:T(8,128)(2,1)S(1)}, bf16[7168,288]{1,0:T(8,128)(2,1)}, u32[]{:S(2)}) %copy-start) | copy-done | bytes 4128792
  18.9 0.0 copy-start.1
  18.9 2.6 %copy-done.1 = bf16[7168,288]{1,0:T(8,128)(2,1)S(1)} copy-done((bf16[7168,288]{1,0:T(8,128)(2,1)S(1)}, bf16[7168,288]{1,0:T(8,128)(2,1)}, u32[]{:S(2)}) %copy-start.1) | copy-done | bytes 4128792
  21.5 32.5 %shard_map.104 = (bf16[2,7168]{1,0:T(2,128)(2,1)S(1)}, bf16[64,288]{1,0:T(8,128)(2,1)S(1)}) custom-call(s32[2]{0:T(128)S(1)} %copy-done.7, bf16[2,7168]{1,0:T(2,128)(2,1)S(1)} %copy-done.6, bf16[2,32,576]{2,1,0:T(8,128)(2,1)S(1)} %copy-done.5, bf16[2,224,576]{2,1,0:T(8,128)(2,1)S(1)} %copy-done.3, bf16[1,512,128]{2,1,0:T(8,128)(2,1)S(1)} %copy-done.4, ...), custom_call_target="tpu_custom_call" | custom-call | tf_op jit(solution)/shard_map/pallas_call | solution.py:335
  54.0 0.6 %copy.18 = bf16[2,7168]{1,0:T(2,128)(2,1)} copy(bf16[2,7168]{1,0:T(2,128)(2,1)S(1)} %get-tuple-element.4) | data formatting | bytes 57344
  54.6 0.6 %copy.19 = bf16[64,288]{1,0:T(8,128)(2,1)} copy(bf16[64,288]{1,0:T(8,128)(2,1)S(1)} %get-tuple-element.5) | data formatting | bytes 73728
Async XLA Ops:
  8.7 7.6 %copy-start.2 = (bf16[128,7168]{1,0:T(8,128)(2,1)S(1)}, bf16[128,7168]{1,0:T(8,128)(2,1)}, u32[]{:S(2)}) copy-start(bf16[128,7168]{1,0:T(8,128)(2,1)} %wout_hbm.1) | copy-start | bytes 5505028
  8.7 7.6 %copy-start.3 = (bf16[2,224,576]{2,1,0:T(8,128)(2,1)S(1)}, bf16[2,224,576]{2,1,0:T(8,128)(2,1)}, u32[]{:S(2)}) copy-start(bf16[2,224,576]{2,1,0:T(8,128)(2,1)} %cache_hbm.1) | copy-start | bytes 1548292
  8.7 7.6 %copy-start.4 = (bf16[1,512,128]{2,1,0:T(8,128)(2,1)S(1)}, bf16[1,512,128]{2,1,0:T(8,128)(2,1)}, u32[]{:S(2)}) copy-start(bf16[1,512,128]{2,1,0:T(8,128)(2,1)} %wuv_hbm.1) | copy-start | bytes 393220
  8.7 7.6 %copy-start.5 = (bf16[2,32,576]{2,1,0:T(8,128)(2,1)S(1)}, bf16[2,32,576]{2,1,0:T(8,128)(2,1)}, u32[]{:S(2)}) copy-start(bf16[2,32,576]{2,1,0:T(8,128)(2,1)} %q_hbm.1) | copy-start | bytes 221188
  8.8 7.6 %copy-start.6 = (bf16[2,7168]{1,0:T(2,128)(2,1)S(1)}, bf16[2,7168]{1,0:T(2,128)(2,1)}, u32[]{:S(2)}) copy-start(bf16[2,7168]{1,0:T(2,128)(2,1)} %hid_hbm.1) | copy-start | bytes 86020
  8.8 7.6 %copy-start.7 = (s32[2]{0:T(128)S(1)}, s32[2]{0:T(128)}, u32[]{:S(2)}) copy-start(s32[2]{0:T(128)} %lengths_ref.1) | copy-start | bytes 28
  16.3 2.6 %copy-start = (bf16[7168,288]{1,0:T(8,128)(2,1)S(1)}, bf16[7168,288]{1,0:T(8,128)(2,1)}, u32[]{:S(2)}) copy-start(bf16[7168,288]{1,0:T(8,128)(2,1)} %copy.14.wg_hbm) | copy-start | bytes 12386308
  18.9 2.6 %copy-start.1 = (bf16[7168,288]{1,0:T(8,128)(2,1)S(1)}, bf16[7168,288]{1,0:T(8,128)(2,1)}, u32[]{:S(2)}) copy-start(bf16[7168,288]{1,0:T(8,128)(2,1)} %copy.15.wu_hbm) | copy-start | bytes 12386308

commit v2 on v1

--- a/solution.py
+++ b/solution.py
@@ -27,11 +27,11 @@
     pieces = latent // LANES
 
     def kernel(
-        lengths_ref, hid_hbm, q_hbm, cache_hbm, wuv_hbm, wout_hbm, gain_ref, wg_hbm, wu_hbm,
+        lengths_hbm, hid_hbm, q_hbm, cache_hbm, wuv_hbm, wout_hbm, gain_hbm, wg_hbm, wu_hbm,
         att_ref, mlp_ref,
-        q_v, cache_v, wuv_v, w2_v, hid_v, wg_v, wu_v, send_perm, recv_perm,
+        lengths_s, q_v, cache_v, wuv_v, w2_v, hid_v, gain_v, gain_f, mlp_v, send_perm, recv_perm,
         ctx_send, ctx_recv, part_v, red_v, x_v,
-        in_sem, w2_sem, hid_sem, w2x_send, w2x_recv, hidx_send, hidx_recv, wuvx_send, wuvx_recv,
+        in_sem, w2_sem, hid_sem, mlp_sem, w2x_send, w2x_recv, hidx_send, hidx_recv, wuvx_send, wuvx_recv,
         ctx_ssem, ctx_rsem, red_ssem, red_rsem, all_ssem, all_rsem, fwd_ssem, fwd_rsem,
     ):
         group = lax.axis_index("group")
@@ -55,8 +55,12 @@
 
         load_cache = pltpu.make_async_copy(cache_hbm, cache_v, in_sem.at[0])
         load_q = pltpu.make_async_copy(q_hbm, q_v, in_sem.at[1])
+        load_lengths = pltpu.make_async_copy(lengths_hbm, lengths_s, in_sem.at[3])
+        load_gain = pltpu.make_async_copy(gain_hbm, gain_v, in_sem.at[4])
         load_cache.start()
         load_q.start()
+        load_lengths.start()
+        load_gain.start()
         barrier = pltpu.get_barrier_semaphore()
         for dx, dy in OFFSETS:
             for dc in range(2):
@@ -86,10 +90,18 @@
             )
         for copy in loads_w2 + loads_hid:
             copy.start()
-        load_wg = pltpu.make_async_copy(wg_hbm, wg_v, in_sem.at[3])
-        load_wu = pltpu.make_async_copy(wu_hbm, wu_v, in_sem.at[4])
-        load_wg.start()
-        load_wu.start()
+        loads_mlp = []
+        for k in range(2 * SIDE):
+            for i, weight in enumerate((wg_hbm, wu_hbm)):
+                loads_mlp.append(
+                    pltpu.make_async_copy(
+                        weight.at[:, pl.ds(k * block, block)],
+                        mlp_v.at[k, pl.ds(i * hidden, hidden)],
+                        mlp_sem.at[2 * k + i],
+                    )
+                )
+        for copy in loads_mlp:
+            copy.start()
 
         size = CHIPS * 16
         row = lax.broadcasted_iota(jnp.int32, (size, size), 0)
@@ -102,6 +114,7 @@
         src_row = (tok // 2) * 16 + (row // 32) * 2 + tok % 2
         recv_perm[...] = (col == src_row).astype(jnp.bfloat16)
 
+        load_lengths.wait()
         load_cache.wait()
         load_q.wait()
         position = lax.broadcasted_iota(jnp.int32, (heads, positions), 1)
@@ -114,7 +127,7 @@
                 )
                 * score_scale
             )
-            visible = position < lengths_ref[r]
+            visible = position < lengths_s[r]
             top = jnp.max(jnp.where(visible, scores, -1e30), axis=-1, keepdims=True)
             probs = jnp.exp(jnp.where(visible, scores - top, -1e30))
             total = jnp.sum(probs, axis=-1, keepdims=True)
@@ -250,23 +263,29 @@
                 copy.start()
                 sends.append(copy)
 
-        load_wg.wait()
-        load_wu.wait()
-        gate = jnp.zeros((tokens, hidden), jnp.float32)
-        up = jnp.zeros((tokens, hidden), jnp.float32)
+        load_gain.wait()
+        gains = gain_v[...].astype(jnp.float32)
+        for k in range(2 * SIDE):
+            for i in range(block // LANES):
+                at = k * (block // LANES) + i
+                gain_f[k, 0:1, i * LANES : (i + 1) * LANES] = gains[at : at + 1, :]
+        for copy in loads_mlp:
+            copy.wait()
+        both = jnp.zeros((tokens, 2 * hidden), jnp.float32)
         square = jnp.zeros((tokens, 1), jnp.float32)
 
         def multiply(which, b, carry):
-            gate, up, square = carry
+            both, square = carry
+            k = which * SIDE + b
             x = x_v[which, b].reshape(tokens, block).astype(jnp.float32)
             square = square + jnp.sum(x * x, axis=-1, keepdims=True)
-            x = (x * gain_ref[which * SIDE + b].astype(jnp.float32)).astype(jnp.bfloat16)
-            span = pl.ds(pl.multiple_of(which * half + b * block, block), block)
-            gate = gate + jnp.dot(x, wg_v[span, :], preferred_element_type=jnp.float32)
-            up = up + jnp.dot(x, wu_v[span, :], preferred_element_type=jnp.float32)
-            return (gate, up, square)
-
-        carry = (gate, up, square)
+            x = (x * gain_f[k]).astype(jnp.bfloat16)
+            both = both + lax.dot_general(
+                x, mlp_v[k], (((1,), (1,)), ((), ())), preferred_element_type=jnp.float32
+            )
+            return (both, square)
+
+        carry = (both, square)
         forwards = []
         for dx in reversed(COLUMN_ORDER):
             b = lax.rem(cx + dx, SIDE)
@@ -290,10 +309,10 @@
                 x_v.at[other, b], x_v.at[other, b], fwd_ssem.at[b], fwd_rsem.at[b], partner
             ).wait_recv()
             carry = multiply(other, b, carry)
-        gate, up, square = carry
-        scale = lax.rsqrt(square / width + 1e-6)
-        gate = gate * scale
-        up = up * scale
+        both, square = carry
+        both = both * lax.rsqrt(square / width + 1e-6)
+        gate = both[:, :hidden]
+        up = both[:, hidden:]
         mlp_ref[...] = (gate / (1.0 + jnp.exp(-gate)) * up).astype(jnp.bfloat16)
 
         first = lax.rem(chip, SIDE) * (2 * req) + core * req
@@ -330,7 +349,7 @@
     size = CHIPS * 16
     bf16 = jnp.bfloat16
     dma = pltpu.SemaphoreType.DMA
-    hbm = pl.BlockSpec(memory_space=pl.ANY)
+    hbm = pl.BlockSpec(memory_space=pltpu.HBM)
     vmem = pl.BlockSpec(memory_space=pltpu.VMEM)
     return pl.pallas_call(
         make_kernel(req, heads, latent, value, rotary, width, hidden, positions),
@@ -338,16 +357,18 @@
             jax.ShapeDtypeStruct((req, width), bf16),
             jax.ShapeDtypeStruct((tokens, hidden), bf16),
         ),
-        in_specs=[pl.BlockSpec(memory_space=pltpu.SMEM), hbm, hbm, hbm, hbm, hbm, vmem, hbm, hbm],
+        in_specs=[hbm] * 9,
         out_specs=(vmem, vmem),
         scratch_shapes=[
+            pltpu.SMEM((req,), jnp.int32),
             pltpu.VMEM((req, heads, depth), bf16),
             pltpu.VMEM((req, positions, depth), bf16),
             pltpu.VMEM((2, latent, value), bf16),
             pltpu.VMEM((SIDE, 2, value, block), bf16),
             pltpu.VMEM((SIDE, 2, req, block), bf16),
-            pltpu.VMEM((width, hidden), bf16),
-            pltpu.VMEM((width, hidden), bf16),
+            pltpu.VMEM((width // LANES, LANES), bf16),
+            pltpu.VMEM((2 * SIDE, 1, block), jnp.float32),
+            pltpu.VMEM((2 * SIDE, 2 * hidden, block), bf16),
             pltpu.VMEM((size, size), bf16),
             pltpu.VMEM((size, size), bf16),
             pltpu.VMEM((CHIPS, 16, LANES), bf16),
@@ -358,6 +379,7 @@
             dma((5,)),
             dma((SIDE,)),
             dma((SIDE,)),
+            dma((4 * SIDE,)),
             dma((SIDE,)),
             dma((SIDE,)),
             dma((SIDE,)),
@@ -374,11 +396,11 @@
             dma((SIDE,)),
         ],
         compiler_params=pltpu.CompilerParams(
-            collective_id=0, has_side_effects=True, vmem_limit_bytes=40 * 1024 * 1024
+            collective_id=0, has_side_effects=True, vmem_limit_bytes=60 * 1024 * 1024
         ),
     )(
         lengths, hidden_in, queries, cache, w_uv, w_out,
-        norm_gain.reshape(2 * SIDE, 1, block), w_gate, w_up,
+        norm_gain.reshape(width // LANES, LANES), w_gate.T, w_up.T,
     )
 
 

time: 55.7 us -> 36.6 us (0.66)
  local copies, waits for them, and re-layouts: 22 us -> 2.8 us
    unnamed x20 -> x2, local copies, waits for them, and re-layouts: 21.3 us -> 2.8 us
    reshape x1 -> x0, local copies, waits for them, and re-layouts: 0.72 us -> none  [per_device(): norm_gain.reshape(2 * SIDE, 1, block)]
where the time goes in v2:
time: 36.6 us; the launch traced here: 36.4 us
  Pallas kernels  33 us (90%)
  local copies, waits for them, and re-layouts  2.8 us (8%)
  between operations  0.64 us (2%)
    pallas_call x1, Pallas kernels, per_device(): pl.pallas_call(make_kernel(req, heads, latent, value, rotary, width, hidd...  33 us
    unnamed x2, local copies, waits for them, and re-layouts  2.8 us

profile of v2, /device:TPU:1, one launch (start us, length us, event | category | flops | bytes accessed | tf_op | source)
XLA Modules:
  0.0 36.4 jit_solution(15989972144890885243)
XLA Ops:
  0.6 33.0 %shard_map.104 = (bf16[2,7168]{1,0:T(2,128)(2,1)}, bf16[64,288]{1,0:T(8,128)(2,1)}) custom-call(s32[2]{0:T(128)} %lengths_hbm.1, bf16[2,7168]{1,0:T(2,128)(2,1)} %hid_hbm.1, bf16[2,32,576]{2,1,0:T(8,128)(2,1)} %q_hbm.1, bf16[2,224,576]{2,1,0:T(8,128)(2,1)} %cache_hbm.1, bf16[1,512,128]{2,1,0:T(8,128)(2,1)} %wuv_hbm.1, bf16[128,7168]{1,0:T(8,128)(2,1)} %wout_hbm.1, ...), custom_call_target="tpu_custom_call" | custom-call | tf_op jit(solution)/shard_map/pallas_call | solution.py:354
  33.6 1.4 %copy.13 = bf16[2,7168]{1,0:T(2,128)(2,1)} copy(bf16[2,7168]{1,0:T(2,128)(2,1)} %get-tuple-element.4) | data formatting | bytes 57344
  35.0 1.4 %copy.14 = bf16[64,288]{1,0:T(8,128)(2,1)} copy(bf16[64,288]{1,0:T(8,128)(2,1)} %get-tuple-element.5) | data formatting | bytes 73728

commit v3 on v2

--- a/solution.py
+++ b/solution.py
@@ -16,6 +16,7 @@
     key=lambda o: -(min(o[0], SIDE - o[0]) + min(o[1], SIDE - o[1])),
 )
 COLUMN_ORDER = (2, 1, 3, 0)
+PIECES = ((0, 256), (256, 512), (512, 896))
 
 
 def make_kernel(req, heads, latent, value, rotary, width, hidden, positions):
@@ -29,7 +30,7 @@
     def kernel(
         lengths_hbm, hid_hbm, q_hbm, cache_hbm, wuv_hbm, wout_hbm, gain_hbm, wg_hbm, wu_hbm,
         att_ref, mlp_ref,
-        lengths_s, q_v, cache_v, wuv_v, w2_v, hid_v, gain_v, gain_f, mlp_v, send_perm, recv_perm,
+        lengths_s, q_v, cache_v, wuv_v, w2_v, hid_v, gain_v, gain_f, wg_v, wu_v, wg_t, wu_t, send_perm, recv_perm,
         ctx_send, ctx_recv, part_v, red_v, x_v,
         in_sem, w2_sem, hid_sem, mlp_sem, w2x_send, w2x_recv, hidx_send, hidx_recv, wuvx_send, wuvx_recv,
         ctx_ssem, ctx_rsem, red_ssem, red_rsem, all_ssem, all_rsem, fwd_ssem, fwd_rsem,
@@ -69,39 +70,6 @@
                     pl.semaphore_signal(
                         barrier, inc=1, device_id=(group, target), device_id_type=MESH
                     )
-        load_wuv = pltpu.make_async_copy(wuv_hbm.at[0], wuv_v.at[core], in_sem.at[2])
-        load_wuv.start()
-
-        def columns(which, b):
-            return pl.ds(pl.multiple_of(which * half + b * block, LANES), block)
-
-        loads_w2 = []
-        loads_hid = []
-        for b in range(SIDE):
-            loads_w2.append(
-                pltpu.make_async_copy(
-                    wout_hbm.at[:, columns(core, b)], w2_v.at[b, core], w2_sem.at[b]
-                )
-            )
-            loads_hid.append(
-                pltpu.make_async_copy(
-                    hid_hbm.at[:, columns(core, b)], hid_v.at[b, core], hid_sem.at[b]
-                )
-            )
-        for copy in loads_w2 + loads_hid:
-            copy.start()
-        loads_mlp = []
-        for k in range(2 * SIDE):
-            for i, weight in enumerate((wg_hbm, wu_hbm)):
-                loads_mlp.append(
-                    pltpu.make_async_copy(
-                        weight.at[:, pl.ds(k * block, block)],
-                        mlp_v.at[k, pl.ds(i * hidden, hidden)],
-                        mlp_sem.at[2 * k + i],
-                    )
-                )
-        for copy in loads_mlp:
-            copy.start()
 
         size = CHIPS * 16
         row = lax.broadcasted_iota(jnp.int32, (size, size), 0)
@@ -117,6 +85,39 @@
         load_lengths.wait()
         load_cache.wait()
         load_q.wait()
+
+        load_wuv = pltpu.make_async_copy(wuv_hbm.at[0], wuv_v.at[core], in_sem.at[2])
+        load_wuv.start()
+
+        def columns(which, b):
+            return pl.ds(pl.multiple_of(which * half + b * block, LANES), block)
+
+        loads_w2 = []
+        loads_hid = []
+        for b in range(SIDE):
+            loads_w2.append(
+                pltpu.make_async_copy(
+                    wout_hbm.at[:, columns(core, b)], w2_v.at[b, core], w2_sem.at[b]
+                )
+            )
+            loads_hid.append(
+                pltpu.make_async_copy(
+                    hid_hbm.at[:, columns(core, b)], hid_v.at[b, core], hid_sem.at[b]
+                )
+            )
+        for copy in loads_w2 + loads_hid:
+            copy.start()
+        loads_mlp = []
+        for k in range(2 * SIDE):
+            for i, (src, dst) in enumerate(((wg_hbm, wg_v), (wu_hbm, wu_v))):
+                loads_mlp.append(
+                    pltpu.make_async_copy(
+                        src.at[:, pl.ds(k * block, block)], dst.at[k], mlp_sem.at[2 * k + i]
+                    )
+                )
+        for copy in loads_mlp:
+            copy.start()
+
         position = lax.broadcasted_iota(jnp.int32, (heads, positions), 1)
         parts = []
         for r in range(req):
@@ -144,6 +145,13 @@
             .astype(jnp.bfloat16)
             .reshape(CHIPS, 16, LANES)
         )
+
+        load_gain.wait()
+        gains = gain_v[...].astype(jnp.float32)
+        for k in range(2 * SIDE):
+            for i in range(block // LANES):
+                at = k * (block // LANES) + i
+                gain_f[k, 0:1, i * LANES : (i + 1) * LANES] = gains[at : at + 1, :]
 
         pl.semaphore_wait(barrier, 2 * CHIPS - 1)
 
@@ -219,6 +227,17 @@
         vals = jnp.concatenate(vals, axis=1)
 
         token = lax.broadcasted_iota(jnp.int32, (tokens, block), 0)
+
+        def reduce_copy(piece, dx, dy):
+            low, high = PIECES[piece]
+            to_chip = chip_at(dx, dy)
+            return remote(
+                part_v.at[lax.rem(cx + dx, SIDE), lax.rem(cy + dy, SIDE), :, low:high],
+                red_v.at[chip, :, low:high],
+                red_ssem.at[piece * CHIPS + to_chip], red_rsem.at[piece * CHIPS + chip],
+                to_chip * 2 + core,
+            )
+
         for dx in COLUMN_ORDER:
             b = lax.rem(cx + dx, SIDE)
             part = jnp.dot(
@@ -233,86 +252,94 @@
             part_v[b] = part.astype(jnp.bfloat16).reshape(SIDE, rows, block)
             for dy in COLUMN_ORDER:
                 if (dx, dy) != (0, 0):
-                    to_chip = chip_at(dx, dy)
-                    copy = remote(
-                        part_v.at[b, lax.rem(cy + dy, SIDE)], red_v.at[chip],
-                        red_ssem.at[to_chip], red_rsem.at[chip], to_chip * 2 + core,
-                    )
+                    copy = reduce_copy(0, dx, dy)
                     copy.start()
                     sends.append(copy)
+        for piece in range(1, len(PIECES)):
+            for dx in COLUMN_ORDER:
+                for dy in COLUMN_ORDER:
+                    if (dx, dy) != (0, 0):
+                        copy = reduce_copy(piece, dx, dy)
+                        copy.start()
+                        sends.append(copy)
         red_v[chip] = part_v[cx, cy]
-        for dx, dy in reversed(OFFSETS):
-            if (dx, dy) != (0, 0):
-                source = chip_at(dx, dy)
-                remote(
-                    part_v.at[0, 0], red_v.at[source],
-                    red_ssem.at[source], red_rsem.at[source], source * 2 + core,
-                ).wait_recv()
-        total = red_v[0].astype(jnp.float32)
-        for k in range(1, CHIPS):
-            total = total + red_v[k].astype(jnp.float32)
-        x_v[core, cx, cy] = total.astype(jnp.bfloat16)
-
-        for dx, dy in OFFSETS:
-            if (dx, dy) != (0, 0):
-                to_chip = chip_at(dx, dy)
-                copy = remote(
-                    x_v.at[core, cx, cy], x_v.at[core, cx, cy],
-                    all_ssem.at[to_chip], all_rsem.at[chip], to_chip * 2 + core,
-                )
+
+        for copy in loads_mlp:
+            copy.wait()
+
+        def turn(k, carry):
+            wg_t[k] = wg_v[k].T
+            wu_t[k] = wu_v[k].T
+            return carry
+
+        lax.fori_loop(0, 2 * SIDE, turn, 0)
+
+        for piece, (low, high) in enumerate(PIECES):
+            for dx, dy in reversed(OFFSETS):
+                if (dx, dy) != (0, 0):
+                    source = chip_at(dx, dy)
+                    at = piece * CHIPS + source
+                    remote(
+                        part_v.at[0, 0, :, low:high], red_v.at[source, :, low:high],
+                        red_ssem.at[at], red_rsem.at[at], source * 2 + core,
+                    ).wait_recv()
+            total = red_v[0, :, low:high].astype(jnp.float32)
+            for k in range(1, CHIPS):
+                total = total + red_v[k, :, low:high].astype(jnp.float32)
+            x_v[core, cx, cy, :, low:high] = total.astype(jnp.bfloat16)
+            for dx, dy in OFFSETS:
+                if (dx, dy) != (0, 0):
+                    to_chip = chip_at(dx, dy)
+                    spot = x_v.at[core, cx, cy, :, low:high]
+                    copy = remote(
+                        spot, spot, all_ssem.at[piece * CHIPS + to_chip],
+                        all_rsem.at[piece * CHIPS + chip], to_chip * 2 + core,
+                    )
+                    copy.start()
+                    sends.append(copy)
+
+        def multiply(which, b, low, high, carry):
+            gate, up, square = carry
+            k = which * SIDE + b
+            x = x_v[which, b, :, :, low:high].reshape(tokens, high - low).astype(jnp.float32)
+            square = square + jnp.sum(x * x, axis=-1, keepdims=True)
+            x = (x * gain_f[k, :, low:high]).astype(jnp.bfloat16)
+            gate = gate + jnp.dot(x, wg_t[k, low:high, :], preferred_element_type=jnp.float32)
+            up = up + jnp.dot(x, wu_t[k, low:high, :], preferred_element_type=jnp.float32)
+            return (gate, up, square)
+
+        carry = (
+            jnp.zeros((tokens, hidden), jnp.float32),
+            jnp.zeros((tokens, hidden), jnp.float32),
+            jnp.zeros((tokens, 1), jnp.float32),
+        )
+        for piece, (low, high) in enumerate(PIECES):
+            for dx in reversed(COLUMN_ORDER):
+                b = lax.rem(cx + dx, SIDE)
+                for dy in reversed(COLUMN_ORDER):
+                    if (dx, dy) != (0, 0):
+                        source = chip_at(dx, dy)
+                        at = piece * CHIPS + source
+                        spot = x_v.at[core, b, lax.rem(cy + dy, SIDE), :, low:high]
+                        remote(
+                            spot, spot, all_ssem.at[at], all_rsem.at[at], source * 2 + core
+                        ).wait_recv()
+                spot = x_v.at[core, b, :, :, low:high]
+                at = piece * SIDE + b
+                copy = remote(spot, spot, fwd_ssem.at[at], fwd_rsem.at[at], partner)
                 copy.start()
                 sends.append(copy)
-
-        load_gain.wait()
-        gains = gain_v[...].astype(jnp.float32)
-        for k in range(2 * SIDE):
-            for i in range(block // LANES):
-                at = k * (block // LANES) + i
-                gain_f[k, 0:1, i * LANES : (i + 1) * LANES] = gains[at : at + 1, :]
-        for copy in loads_mlp:
-            copy.wait()
-        both = jnp.zeros((tokens, 2 * hidden), jnp.float32)
-        square = jnp.zeros((tokens, 1), jnp.float32)
-
-        def multiply(which, b, carry):
-            both, square = carry
-            k = which * SIDE + b
-            x = x_v[which, b].reshape(tokens, block).astype(jnp.float32)
-            square = square + jnp.sum(x * x, axis=-1, keepdims=True)
-            x = (x * gain_f[k]).astype(jnp.bfloat16)
-            both = both + lax.dot_general(
-                x, mlp_v[k], (((1,), (1,)), ((), ())), preferred_element_type=jnp.float32
-            )
-            return (both, square)
-
-        carry = (both, square)
-        forwards = []
-        for dx in reversed(COLUMN_ORDER):
-            b = lax.rem(cx + dx, SIDE)
-            for dy in reversed(COLUMN_ORDER):
-                if (dx, dy) != (0, 0):
-                    source = chip_at(dx, dy)
-                    a = lax.rem(cy + dy, SIDE)
-                    remote(
-                        x_v.at[core, b, a], x_v.at[core, b, a],
-                        all_ssem.at[source], all_rsem.at[source], source * 2 + core,
-                    ).wait_recv()
-            copy = remote(
-                x_v.at[core, b], x_v.at[core, b], fwd_ssem.at[b], fwd_rsem.at[b], partner
-            )
-            copy.start()
-            sends.append(copy)
-            carry = multiply(core, b, carry)
-        for dx in reversed(COLUMN_ORDER):
-            b = lax.rem(cx + dx, SIDE)
-            remote(
-                x_v.at[other, b], x_v.at[other, b], fwd_ssem.at[b], fwd_rsem.at[b], partner
-            ).wait_recv()
-            carry = multiply(other, b, carry)
-        both, square = carry
-        both = both * lax.rsqrt(square / width + 1e-6)
-        gate = both[:, :hidden]
-        up = both[:, hidden:]
+                carry = multiply(core, b, low, high, carry)
+            for dx in reversed(COLUMN_ORDER):
+                b = lax.rem(cx + dx, SIDE)
+                spot = x_v.at[other, b, :, :, low:high]
+                at = piece * SIDE + b
+                remote(spot, spot, fwd_ssem.at[at], fwd_rsem.at[at], partner).wait_recv()
+                carry = multiply(other, b, low, high, carry)
+        gate, up, square = carry
+        scale = lax.rsqrt(square / width + 1e-6)
+        gate = gate * scale
+        up = up * scale
         mlp_ref[...] = (gate / (1.0 + jnp.exp(-gate)) * up).astype(jnp.bfloat16)
 
         first = lax.rem(chip, SIDE) * (2 * req) + core * req
@@ -334,6 +361,17 @@
             copy.wait_send()
 
     return kernel
+
+
+def write_out(att_ref, mlp_ref, att_hbm, mlp_hbm, sem):
+    copies = (
+        pltpu.make_async_copy(att_ref, att_hbm, sem.at[0]),
+        pltpu.make_async_copy(mlp_ref, mlp_hbm, sem.at[1]),
+    )
+    for copy in copies:
+        copy.start()
+    for copy in copies:
+        copy.wait()
 
 
 def per_device(hidden_in, queries, cache, lengths, w_uv, w_out, norm_gain, w_gate, w_up):
@@ -351,12 +389,13 @@
     dma = pltpu.SemaphoreType.DMA
     hbm = pl.BlockSpec(memory_space=pltpu.HBM)
     vmem = pl.BlockSpec(memory_space=pltpu.VMEM)
-    return pl.pallas_call(
+    outs = (
+        jax.ShapeDtypeStruct((req, width), bf16),
+        jax.ShapeDtypeStruct((tokens, hidden), bf16),
+    )
+    att, mlp = pl.pallas_call(
         make_kernel(req, heads, latent, value, rotary, width, hidden, positions),
-        out_shape=(
-            jax.ShapeDtypeStruct((req, width), bf16),
-            jax.ShapeDtypeStruct((tokens, hidden), bf16),
-        ),
+        out_shape=outs,
         in_specs=[hbm] * 9,
         out_specs=(vmem, vmem),
         scratch_shapes=[
@@ -368,7 +407,10 @@
             pltpu.VMEM((SIDE, 2, req, block), bf16),
             pltpu.VMEM((width // LANES, LANES), bf16),
             pltpu.VMEM((2 * SIDE, 1, block), jnp.float32),
-            pltpu.VMEM((2 * SIDE, 2 * hidden, block), bf16),
+            pltpu.VMEM((2 * SIDE, hidden, block), bf16),
+            pltpu.VMEM((2 * SIDE, hidden, block), bf16),
+            pltpu.VMEM((2 * SIDE, block, hidden), bf16),
+            pltpu.VMEM((2 * SIDE, block, hidden), bf16),
             pltpu.VMEM((size, size), bf16),
             pltpu.VMEM((size, size), bf16),
             pltpu.VMEM((CHIPS, 16, LANES), bf16),
@@ -388,20 +430,33 @@
             dma((1,)),
             dma((2 * CHIPS,)),
             dma((2 * CHIPS,)),
-            dma((CHIPS,)),
-            dma((CHIPS,)),
-            dma((CHIPS,)),
-            dma((CHIPS,)),
-            dma((SIDE,)),
-            dma((SIDE,)),
+            dma((len(PIECES) * CHIPS,)),
+            dma((len(PIECES) * CHIPS,)),
+            dma((len(PIECES) * CHIPS,)),
+            dma((len(PIECES) * CHIPS,)),
+            dma((len(PIECES) * SIDE,)),
+            dma((len(PIECES) * SIDE,)),
         ],
         compiler_params=pltpu.CompilerParams(
-            collective_id=0, has_side_effects=True, vmem_limit_bytes=60 * 1024 * 1024
+            collective_id=0, has_side_effects=True, vmem_limit_bytes=40 * 1024 * 1024
         ),
     )(
-        lengths, hidden_in, queries, cache, w_uv, w_out,
-        norm_gain.reshape(width // LANES, LANES), w_gate.T, w_up.T,
+        *(
+            pltpu.with_memory_space_constraint(operand, pltpu.HBM)
+            for operand in (
+                lengths, hidden_in, queries, cache, w_uv, w_out,
+                norm_gain.reshape(width // LANES, LANES), w_gate.T, w_up.T,
+            )
+        )
     )
+    return pl.pallas_call(
+        write_out,
+        out_shape=outs,
+        in_specs=[vmem, vmem],
+        out_specs=(hbm, hbm),
+        scratch_shapes=[dma((2,))],
+        compiler_params=pltpu.CompilerParams(vmem_limit_bytes=1024 * 1024),
+    )(att, mlp)
 
 
 def solution(mesh):

time: 36.6 us -> 32.5 us (0.89)
  local copies, waits for them, and re-layouts: 2.8 us -> 0 us
  Pallas kernels: 33 us -> 31.7 us
    unnamed x2 -> x0, local copies, waits for them, and re-layouts: 2.8 us -> none
    pallas_call x1, Pallas kernels: 33 us -> 31.1 us  [per_device(): pl.pallas_call(make_kernel(req, heads, latent, value, rotary, width, hidd...]
    pallas_call x0 -> x1, Pallas kernels: none -> 0.65 us  [per_device(): pl.pallas_call(write_out, out_shape=outs, in_specs=[vmem, vmem], out_spec...]
where the time goes in v3:
time: 32.5 us; the launch traced here: 32.4 us
  Pallas kernels  31.7 us (98%)
  between operations  0.64 us (2%)
    pallas_call x1, Pallas kernels, per_device(): pl.pallas_call(make_kernel(req, heads, latent, value, rotary, width, hidd...  31.1 us

profile of v3, /device:TPU:1, one launch (start us, length us, event | category | flops | bytes accessed | tf_op | source)
XLA Modules:
  0.0 32.4 jit_solution(2304106398742435374)
XLA Ops:
  0.6 31.1 %shard_map.104 = (bf16[2,7168]{1,0:T(2,128)(2,1)S(1)}, bf16[64,288]{1,0:T(8,128)(2,1)S(1)}) custom-call(s32[2]{0:T(128)} %lengths_hbm.1, bf16[2,7168]{1,0:T(2,128)(2,1)} %hid_hbm.1, bf16[2,32,576]{2,1,0:T(8,128)(2,1)} %q_hbm.1, bf16[2,224,576]{2,1,0:T(8,128)(2,1)} %cache_hbm.1, bf16[1,512,128]{2,1,0:T(8,128)(2,1)} %wuv_hbm.1, bf16[128,7168]{1,0:T(8,128)(2,1)} %wout_hbm.1, ...), custom_call_target="tpu_custom_call" | custom-call | tf_op jit(solution)/shard_map/pallas_call | solution.py:396
  31.7 0.6 %shard_map.105 = (bf16[2,7168]{1,0:T(2,128)(2,1)}, bf16[64,288]{1,0:T(8,128)(2,1)}) custom-call(bf16[2,7168]{1,0:T(2,128)(2,1)S(1)} %get-tuple-element.4.att_ref, bf16[64,288]{1,0:T(8,128)(2,1)S(1)} %get-tuple-element.5.mlp_ref), custom_call_target="tpu_custom_call" | custom-call | tf_op jit(solution)/shard_map/pallas_call | solution.py:452

commit v4 on v3

--- a/solution.py
+++ b/solution.py
@@ -86,38 +86,6 @@
         load_cache.wait()
         load_q.wait()
 
-        load_wuv = pltpu.make_async_copy(wuv_hbm.at[0], wuv_v.at[core], in_sem.at[2])
-        load_wuv.start()
-
-        def columns(which, b):
-            return pl.ds(pl.multiple_of(which * half + b * block, LANES), block)
-
-        loads_w2 = []
-        loads_hid = []
-        for b in range(SIDE):
-            loads_w2.append(
-                pltpu.make_async_copy(
-                    wout_hbm.at[:, columns(core, b)], w2_v.at[b, core], w2_sem.at[b]
-                )
-            )
-            loads_hid.append(
-                pltpu.make_async_copy(
-                    hid_hbm.at[:, columns(core, b)], hid_v.at[b, core], hid_sem.at[b]
-                )
-            )
-        for copy in loads_w2 + loads_hid:
-            copy.start()
-        loads_mlp = []
-        for k in range(2 * SIDE):
-            for i, (src, dst) in enumerate(((wg_hbm, wg_v), (wu_hbm, wu_v))):
-                loads_mlp.append(
-                    pltpu.make_async_copy(
-                        src.at[:, pl.ds(k * block, block)], dst.at[k], mlp_sem.at[2 * k + i]
-                    )
-                )
-        for copy in loads_mlp:
-            copy.start()
-
         position = lax.broadcasted_iota(jnp.int32, (heads, positions), 1)
         parts = []
         for r in range(req):
@@ -155,7 +123,6 @@
 
         pl.semaphore_wait(barrier, 2 * CHIPS - 1)
 
-        sends = []
         for dx, dy in OFFSETS:
             for dc in range(2):
                 if (dx, dy, dc) != (0, 0, 0):
@@ -163,46 +130,49 @@
                     target = to_chip * 2 + lax.rem(core + dc, 2)
                     copy = remote(
                         ctx_send.at[to_chip], ctx_recv.at[me],
-                        ctx_ssem.at[target], ctx_rsem.at[me], target,
+                        ctx_ssem.at[0], ctx_rsem.at[0], target,
                     )
                     copy.start()
-                    sends.append(copy)
+        def half_of(which):
+            return pl.ds(pl.multiple_of(which * half, LANES), half)
+
+        load_w2 = pltpu.make_async_copy(wout_hbm.at[:, half_of(core)], w2_v.at[core], w2_sem.at[0])
+        trade_w2 = remote(
+            wout_hbm.at[:, half_of(other)], w2_v.at[core], w2x_send.at[0], w2x_recv.at[0], partner
+        )
+        load_wuv = pltpu.make_async_copy(wuv_hbm.at[0], wuv_v.at[core], in_sem.at[2])
         trade_wuv = remote(
             wuv_hbm.at[0], wuv_v.at[core], wuvx_send.at[0], wuvx_recv.at[0], partner
         )
-        trade_wuv.start()
-        trade_w2 = []
-        trade_hid = []
-        for b in range(SIDE):
-            trade_w2.append(
-                remote(
-                    wout_hbm.at[:, columns(other, b)], w2_v.at[b, core],
-                    w2x_send.at[b], w2x_recv.at[b], partner,
+        load_hid = pltpu.make_async_copy(
+            hid_hbm.at[:, half_of(core)], hid_v.at[core], hid_sem.at[0]
+        )
+        trade_hid = remote(
+            hid_hbm.at[:, half_of(other)], hid_v.at[core], hidx_send.at[0], hidx_recv.at[0], partner
+        )
+        loads = (load_wuv, load_w2, load_hid)
+        trades = (trade_wuv, trade_w2, trade_hid)
+        for copy in trades + loads:
+            copy.start()
+        loads_mlp = []
+        for k in range(2 * SIDE):
+            for i, (src, dst) in enumerate(((wg_hbm, wg_v), (wu_hbm, wu_v))):
+                loads_mlp.append(
+                    pltpu.make_async_copy(
+                        src.at[:, pl.ds(k * block, block)], dst.at[k], mlp_sem.at[2 * k + i]
+                    )
                 )
-            )
-            trade_hid.append(
-                remote(
-                    hid_hbm.at[:, columns(other, b)], hid_v.at[b, core],
-                    hidx_send.at[b], hidx_recv.at[b], partner,
-                )
-            )
-        for copy in trade_w2 + trade_hid:
+        for copy in loads_mlp:
             copy.start()
         ctx_recv[me] = ctx_send[chip]
 
-        for copy in [load_wuv] + loads_w2 + loads_hid:
+        for copy in loads:
             copy.wait()
-        trade_wuv.wait_recv()
-        for copy in trade_w2 + trade_hid:
+        for copy in trades:
             copy.wait_recv()
-        for dx, dy in reversed(OFFSETS):
-            for dc in range(2):
-                if (dx, dy, dc) != (0, 0, 0):
-                    source = chip_at(dx, dy) * 2 + lax.rem(core + dc, 2)
-                    remote(
-                        ctx_send.at[0], ctx_recv.at[source],
-                        ctx_ssem.at[source], ctx_rsem.at[source], source,
-                    ).wait_recv()
+        others = ctx_recv.at[pl.ds(0, 2 * CHIPS - 1)]
+        all_ctx = remote(others, others, ctx_ssem.at[0], ctx_rsem.at[0], partner)
+        all_ctx.wait_recv()
 
         got = ctx_recv[...].reshape(2, size, LANES)
         ordered = [
@@ -229,40 +199,44 @@
         token = lax.broadcasted_iota(jnp.int32, (tokens, block), 0)
 
         def reduce_copy(piece, dx, dy):
-            low, high = PIECES[piece]
             to_chip = chip_at(dx, dy)
             return remote(
-                part_v.at[lax.rem(cx + dx, SIDE), lax.rem(cy + dy, SIDE), :, low:high],
-                red_v.at[chip, :, low:high],
-                red_ssem.at[piece * CHIPS + to_chip], red_rsem.at[piece * CHIPS + chip],
+                part_v[piece].at[lax.rem(cx + dx, SIDE), lax.rem(cy + dy, SIDE)],
+                red_v[piece].at[chip],
+                red_ssem.at[piece], red_rsem.at[piece],
                 to_chip * 2 + core,
             )
+
+        def fifteen(piece, ssem, rsem):
+            others = red_v[piece].at[pl.ds(0, CHIPS - 1)]
+            return remote(others, others, ssem.at[piece], rsem.at[piece], partner)
 
         for dx in COLUMN_ORDER:
             b = lax.rem(cx + dx, SIDE)
+            span = pl.ds(pl.multiple_of(b * block, LANES), block)
             part = jnp.dot(
-                vals, w2_v[b].reshape(2 * value, block), preferred_element_type=jnp.float32
-            )
-            own = hid_v[b].astype(jnp.float32)
+                vals, w2_v[:, :, span].reshape(2 * value, block), preferred_element_type=jnp.float32
+            )
+            own = hid_v[:, :, span].astype(jnp.float32)
             for h in range(2):
                 for r in range(req):
                     part = part + jnp.where(
                         token == chip * (2 * req) + h * req + r, own[h, r : r + 1, :], 0.0
                     )
-            part_v[b] = part.astype(jnp.bfloat16).reshape(SIDE, rows, block)
+            for piece, (low, high) in enumerate(PIECES):
+                part_v[piece][b] = (
+                    part[:, low:high].astype(jnp.bfloat16).reshape(SIDE, rows, high - low)
+                )
             for dy in COLUMN_ORDER:
                 if (dx, dy) != (0, 0):
-                    copy = reduce_copy(0, dx, dy)
-                    copy.start()
-                    sends.append(copy)
+                    reduce_copy(0, dx, dy).start()
         for piece in range(1, len(PIECES)):
             for dx in COLUMN_ORDER:
                 for dy in COLUMN_ORDER:
                     if (dx, dy) != (0, 0):
-                        copy = reduce_copy(piece, dx, dy)
-                        copy.start()
-                        sends.append(copy)
-        red_v[chip] = part_v[cx, cy]
+                        reduce_copy(piece, dx, dy).start()
+        for part, red in zip(part_v, red_v):
+            red[chip] = part[cx, cy]
 
         for copy in loads_mlp:
             copy.wait()
@@ -273,35 +247,31 @@
             return carry
 
         lax.fori_loop(0, 2 * SIDE, turn, 0)
-
-        for piece, (low, high) in enumerate(PIECES):
-            for dx, dy in reversed(OFFSETS):
-                if (dx, dy) != (0, 0):
-                    source = chip_at(dx, dy)
-                    at = piece * CHIPS + source
-                    remote(
-                        part_v.at[0, 0, :, low:high], red_v.at[source, :, low:high],
-                        red_ssem.at[at], red_rsem.at[at], source * 2 + core,
-                    ).wait_recv()
-            total = red_v[0, :, low:high].astype(jnp.float32)
+        all_ctx.wait_send()
+        for copy in trades:
+            copy.wait_send()
+
+        for piece in range(len(PIECES)):
+            fifteen(piece, red_ssem, red_rsem).wait_recv()
+            total = red_v[piece][0].astype(jnp.float32)
             for k in range(1, CHIPS):
-                total = total + red_v[k, :, low:high].astype(jnp.float32)
-            x_v[core, cx, cy, :, low:high] = total.astype(jnp.bfloat16)
+                total = total + red_v[piece][k].astype(jnp.float32)
+            x_v[piece][core, cx, cy] = total.astype(jnp.bfloat16)
             for dx, dy in OFFSETS:
                 if (dx, dy) != (0, 0):
                     to_chip = chip_at(dx, dy)
-                    spot = x_v.at[core, cx, cy, :, low:high]
+                    spot = x_v[piece].at[core, cx, cy]
                     copy = remote(
-                        spot, spot, all_ssem.at[piece * CHIPS + to_chip],
-                        all_rsem.at[piece * CHIPS + chip], to_chip * 2 + core,
+                        spot, spot, all_ssem.at[piece],
+                        all_rsem.at[piece], to_chip * 2 + core,
                     )
                     copy.start()
-                    sends.append(copy)
-
-        def multiply(which, b, low, high, carry):
+
+        def multiply(which, b, piece, carry):
+            low, high = PIECES[piece]
             gate, up, square = carry
             k = which * SIDE + b
-            x = x_v[which, b, :, :, low:high].reshape(tokens, high - low).astype(jnp.float32)
+            x = x_v[piece][which, b].reshape(tokens, high - low).astype(jnp.float32)
             square = square + jnp.sum(x * x, axis=-1, keepdims=True)
             x = (x * gain_f[k, :, low:high]).astype(jnp.bfloat16)
             gate = gate + jnp.dot(x, wg_t[k, low:high, :], preferred_element_type=jnp.float32)
@@ -313,52 +283,61 @@
             jnp.zeros((tokens, hidden), jnp.float32),
             jnp.zeros((tokens, 1), jnp.float32),
         )
-        for piece, (low, high) in enumerate(PIECES):
-            for dx in reversed(COLUMN_ORDER):
-                b = lax.rem(cx + dx, SIDE)
-                for dy in reversed(COLUMN_ORDER):
-                    if (dx, dy) != (0, 0):
-                        source = chip_at(dx, dy)
-                        at = piece * CHIPS + source
-                        spot = x_v.at[core, b, lax.rem(cy + dy, SIDE), :, low:high]
-                        remote(
-                            spot, spot, all_ssem.at[at], all_rsem.at[at], source * 2 + core
-                        ).wait_recv()
-                spot = x_v.at[core, b, :, :, low:high]
-                at = piece * SIDE + b
-                copy = remote(spot, spot, fwd_ssem.at[at], fwd_rsem.at[at], partner)
-                copy.start()
-                sends.append(copy)
-                carry = multiply(core, b, low, high, carry)
-            for dx in reversed(COLUMN_ORDER):
-                b = lax.rem(cx + dx, SIDE)
-                spot = x_v.at[other, b, :, :, low:high]
-                at = piece * SIDE + b
-                remote(spot, spot, fwd_ssem.at[at], fwd_rsem.at[at], partner).wait_recv()
-                carry = multiply(other, b, low, high, carry)
+        def forward(piece, which):
+            spot = x_v[piece].at[which]
+            return remote(spot, spot, fwd_ssem.at[piece], fwd_rsem.at[piece], partner)
+
+        def own_blocks(piece, carry):
+            fifteen(piece, all_ssem, all_rsem).wait_recv()
+            forward(piece, core).start()
+            for b in range(SIDE):
+                carry = multiply(core, b, piece, carry)
+            return carry
+
+        def partner_blocks(piece, carry):
+            forward(piece, other).wait_recv()
+            for b in range(SIDE):
+                carry = multiply(other, b, piece, carry)
+            return carry
+
+        first = lax.rem(chip, SIDE) * (2 * req) + core * req
+
+        def keep_rows(which, piece):
+            low, high = PIECES[piece]
+            line = lax.broadcasted_iota(jnp.int32, (rows, high - low), 0)
+            for b in range(SIDE):
+                x = x_v[piece][which, b, cy].astype(jnp.float32)
+                picked = [
+                    jnp.sum(jnp.where(line == first + r, x, 0.0), axis=0, keepdims=True)
+                    for r in range(req)
+                ]
+                at = pl.multiple_of(which * half + b * block + low, LANES)
+                att_ref[:, pl.ds(at, high - low)] = jnp.concatenate(picked, axis=0).astype(
+                    jnp.bfloat16
+                )
+
+        for piece in range(len(PIECES)):
+            fifteen(piece, red_ssem, red_rsem).wait_send()
+        last = len(PIECES) - 1
+        for piece in range(last + 1):
+            carry = own_blocks(piece, carry)
+            if piece > 0:
+                carry = partner_blocks(piece - 1, carry)
+                keep_rows(other, piece - 1)
+            keep_rows(core, piece)
+        carry = partner_blocks(last, carry)
         gate, up, square = carry
         scale = lax.rsqrt(square / width + 1e-6)
         gate = gate * scale
         up = up * scale
         mlp_ref[...] = (gate / (1.0 + jnp.exp(-gate)) * up).astype(jnp.bfloat16)
 
-        first = lax.rem(chip, SIDE) * (2 * req) + core * req
-        line = lax.broadcasted_iota(jnp.int32, (rows, block), 0)
-        for which in range(2):
-            for b in range(SIDE):
-                x = x_v[which, b, cy].astype(jnp.float32)
-                picked = jnp.concatenate(
-                    [
-                        jnp.sum(jnp.where(line == first + r, x, 0.0), axis=0, keepdims=True)
-                        for r in range(req)
-                    ],
-                    axis=0,
-                )
-                at = which * half + b * block
-                att_ref[:, at : at + block] = picked.astype(jnp.bfloat16)
-
-        for copy in sends + [trade_wuv] + trade_w2 + trade_hid:
-            copy.wait_send()
+        keep_rows(other, last)
+
+        for piece in range(len(PIECES)):
+            fifteen(piece, all_ssem, red_rsem).wait_send()
+        for piece in range(len(PIECES)):
+            forward(piece, core).wait_send()
 
     return kernel
 
@@ -403,8 +382,8 @@
             pltpu.VMEM((req, heads, depth), bf16),
             pltpu.VMEM((req, positions, depth), bf16),
             pltpu.VMEM((2, latent, value), bf16),
-            pltpu.VMEM((SIDE, 2, value, block), bf16),
-            pltpu.VMEM((SIDE, 2, req, block), bf16),
+            pltpu.VMEM((2, value, half), bf16),
+            pltpu.VMEM((2, req, half), bf16),
             pltpu.VMEM((width // LANES, LANES), bf16),
             pltpu.VMEM((2 * SIDE, 1, block), jnp.float32),
             pltpu.VMEM((2 * SIDE, hidden, block), bf16),
@@ -415,27 +394,27 @@
             pltpu.VMEM((size, size), bf16),
             pltpu.VMEM((CHIPS, 16, LANES), bf16),
             pltpu.VMEM((2 * CHIPS, 16, LANES), bf16),
-            pltpu.VMEM((SIDE, SIDE, rows, block), bf16),
-            pltpu.VMEM((CHIPS, rows, block), bf16),
-            pltpu.VMEM((2, SIDE, SIDE, rows, block), bf16),
+            [pltpu.VMEM((SIDE, SIDE, rows, high - low), bf16) for low, high in PIECES],
+            [pltpu.VMEM((CHIPS, rows, high - low), bf16) for low, high in PIECES],
+            [pltpu.VMEM((2, SIDE, SIDE, rows, high - low), bf16) for low, high in PIECES],
             dma((5,)),
-            dma((SIDE,)),
-            dma((SIDE,)),
+            dma((1,)),
+            dma((1,)),
             dma((4 * SIDE,)),
-            dma((SIDE,)),
-            dma((SIDE,)),
-            dma((SIDE,)),
-            dma((SIDE,)),
-            dma((1,)),
-            dma((1,)),
-            dma((2 * CHIPS,)),
-            dma((2 * CHIPS,)),
-            dma((len(PIECES) * CHIPS,)),
-            dma((len(PIECES) * CHIPS,)),
-            dma((len(PIECES) * CHIPS,)),
-            dma((len(PIECES) * CHIPS,)),
-            dma((len(PIECES) * SIDE,)),
-            dma((len(PIECES) * SIDE,)),
+            dma((1,)),
+            dma((1,)),
+            dma((1,)),
+            dma((1,)),
+            dma((1,)),
+            dma((1,)),
+            dma((1,)),
+            dma((1,)),
+            dma((len(PIECES),)),
+            dma((len(PIECES),)),
+            dma((len(PIECES),)),
+            dma((len(PIECES),)),
+            dma((len(PIECES),)),
+            dma((len(PIECES),)),
         ],
         compiler_params=pltpu.CompilerParams(
             collective_id=0, has_side_effects=True, vmem_limit_bytes=40 * 1024 * 1024

time: 32.5 us -> 29.6 us (0.911)
  Pallas kernels: 31.7 us -> 28.9 us
    pallas_call x1, Pallas kernels: 31.1 us -> 28.2 us  [per_device(): pl.pallas_call(make_kernel(req, heads, latent, value, rotary, width, hidd...]
where the time goes in v4:
time: 29.6 us; the launch traced here: 29.5 us
  Pallas kernels  28.9 us (98%)
  between operations  0.64 us (2%)
    pallas_call x1, Pallas kernels, per_device(): pl.pallas_call(make_kernel(req, heads, latent, value, rotary, width, hidd...  28.2 us
    pallas_call x1, Pallas kernels, per_device(): pl.pallas_call(write_out, out_shape=outs, in_specs=[vmem, vmem], out_spec...  0.65 us

profile of v4, /device:TPU:1, one launch (start us, length us, event | category | flops | bytes accessed | tf_op | source)
XLA Modules:
  0.0 29.5 jit_solution(15580537250502520054)
XLA Ops:
  0.6 28.2 %shard_map.104 = (bf16[2,7168]{1,0:T(2,128)(2,1)S(1)}, bf16[64,288]{1,0:T(8,128)(2,1)S(1)}) custom-call(s32[2]{0:T(128)} %lengths_hbm.1, bf16[2,7168]{1,0:T(2,128)(2,1)} %hid_hbm.1, bf16[2,32,576]{2,1,0:T(8,128)(2,1)} %q_hbm.1, bf16[2,224,576]{2,1,0:T(8,128)(2,1)} %cache_hbm.1, bf16[1,512,128]{2,1,0:T(8,128)(2,1)} %wuv_hbm.1, bf16[128,7168]{1,0:T(8,128)(2,1)} %wout_hbm.1, ...), custom_call_target="tpu_custom_call" | custom-call | tf_op jit(solution)/shard_map/pallas_call | solution.py:375
  28.9 0.6 %shard_map.105 = (bf16[2,7168]{1,0:T(2,128)(2,1)}, bf16[64,288]{1,0:T(8,128)(2,1)}) custom-call(bf16[2,7168]{1,0:T(2,128)(2,1)S(1)} %get-tuple-element.4.att_ref, bf16[64,288]{1,0:T(8,128)(2,1)S(1)} %get-tuple-element.5.mlp_ref), custom_call_target="tpu_custom_call" | custom-call | tf_op jit(solution)/shard_map/pallas_call | solution.py:431

commit v5 on v4

--- a/solution.py
+++ b/solution.py
@@ -16,7 +16,7 @@
     key=lambda o: -(min(o[0], SIDE - o[0]) + min(o[1], SIDE - o[1])),
 )
 COLUMN_ORDER = (2, 1, 3, 0)
-PIECES = ((0, 256), (256, 512), (512, 896))
+PIECES = ((0, 256), (256, 512), (512, 768), (768, 896))
 
 
 def make_kernel(req, heads, latent, value, rotary, width, hidden, positions):

time: 29.6 us -> 29.1 us (0.983)
  Pallas kernels: 28.9 us -> 28.4 us
    pallas_call x1, Pallas kernels: 28.2 us -> 27.7 us  [per_device(): pl.pallas_call(make_kernel(req, heads, latent, value, rotary, width, hidd...]
where the time goes in v5:
time: 29.1 us; the launch traced here: 29 us
  Pallas kernels  28.4 us (98%)
  between operations  0.64 us (2%)
    pallas_call x1, Pallas kernels, per_device(): pl.pallas_call(make_kernel(req, heads, latent, value, rotary, width, hidd...  27.7 us
    pallas_call x1, Pallas kernels, per_device(): pl.pallas_call(write_out, out_shape=outs, in_specs=[vmem, vmem], out_spec...  0.65 us

profile of v5, /device:TPU:1, one launch (start us, length us, event | category | flops | bytes accessed | tf_op | source)
XLA Modules:
  0.0 29.0 jit_solution(2561606434658164564)
XLA Ops:
  0.6 27.7 %shard_map.104 = (bf16[2,7168]{1,0:T(2,128)(2,1)S(1)}, bf16[64,288]{1,0:T(8,128)(2,1)S(1)}) custom-call(s32[2]{0:T(128)} %lengths_hbm.1, bf16[2,7168]{1,0:T(2,128)(2,1)} %hid_hbm.1, bf16[2,32,576]{2,1,0:T(8,128)(2,1)} %q_hbm.1, bf16[2,224,576]{2,1,0:T(8,128)(2,1)} %cache_hbm.1, bf16[1,512,128]{2,1,0:T(8,128)(2,1)} %wuv_hbm.1, bf16[128,7168]{1,0:T(8,128)(2,1)} %wout_hbm.1, ...), custom_call_target="tpu_custom_call" | custom-call | tf_op jit(solution)/shard_map/pallas_call | solution.py:375
  28.4 0.6 %shard_map.105 = (bf16[2,7168]{1,0:T(2,128)(2,1)}, bf16[64,288]{1,0:T(8,128)(2,1)}) custom-call(bf16[2,7168]{1,0:T(2,128)(2,1)S(1)} %get-tuple-element.4.att_ref, bf16[64,288]{1,0:T(8,128)(2,1)S(1)} %get-tuple-element.5.mlp_ref), custom_call_target="tpu_custom_call" | custom-call | tf_op jit(solution)/shard_map/pallas_call | solution.py:431

commit v6 on v5

--- a/solution.py
+++ b/solution.py
@@ -266,6 +266,13 @@
                         all_rsem.at[piece], to_chip * 2 + core,
                     )
                     copy.start()
+            if piece == len(PIECES) - 1:
+                for dx, dy in OFFSETS:
+                    spot = x_v[piece].at[core, cx, cy]
+                    remote(
+                        spot, spot, fwd_ssem.at[piece], fwd_rsem.at[piece],
+                        chip_at(dx, dy) * 2 + other,
+                    ).start()
 
         def multiply(which, b, piece, carry):
             low, high = PIECES[piece]
@@ -289,7 +296,8 @@
 
         def own_blocks(piece, carry):
             fifteen(piece, all_ssem, all_rsem).wait_recv()
-            forward(piece, core).start()
+            if piece < len(PIECES) - 1:
+                forward(piece, core).start()
             for b in range(SIDE):
                 carry = multiply(core, b, piece, carry)
             return carry

time: 29.1 us -> 29 us (level)
  no operation moved by 1% of the time
where the time goes in v6:
time: 29 us; the launch traced here: 28.9 us
  Pallas kernels  28.2 us (97%)
  between operations  0.64 us (2%)
    pallas_call x1, Pallas kernels, per_device(): pl.pallas_call(make_kernel(req, heads, latent, value, rotary, width, hidd...  27.6 us
    pallas_call x1, Pallas kernels, per_device(): pl.pallas_call(write_out, out_shape=outs, in_specs=[vmem, vmem], out_spec...  0.65 us

profile of v6, /device:TPU:1, one launch (start us, length us, event | category | flops | bytes accessed | tf_op | source)
XLA Modules:
  0.0 28.9 jit_solution(4766849988467014285)
XLA Ops:
  0.6 27.6 %shard_map.104 = (bf16[2,7168]{1,0:T(2,128)(2,1)S(1)}, bf16[64,288]{1,0:T(8,128)(2,1)S(1)}) custom-call(s32[2]{0:T(128)} %lengths_hbm.1, bf16[2,7168]{1,0:T(2,128)(2,1)} %hid_hbm.1, bf16[2,32,576]{2,1,0:T(8,128)(2,1)} %q_hbm.1, bf16[2,224,576]{2,1,0:T(8,128)(2,1)} %cache_hbm.1, bf16[1,512,128]{2,1,0:T(8,128)(2,1)} %wuv_hbm.1, bf16[128,7168]{1,0:T(8,128)(2,1)} %wout_hbm.1, ...), custom_call_target="tpu_custom_call" | custom-call | tf_op jit(solution)/shard_map/pallas_call | solution.py:383
  28.2 0.6 %shard_map.105 = (bf16[2,7168]{1,0:T(2,128)(2,1)}, bf16[64,288]{1,0:T(8,128)(2,1)}) custom-call(bf16[2,7168]{1,0:T(2,128)(2,1)S(1)} %get-tuple-element.4.att_ref, bf16[64,288]{1,0:T(8,128)(2,1)S(1)} %get-tuple-element.5.mlp_ref), custom_call_target="tpu_custom_call" | custom-call | tf_op jit(solution)/shard_map/pallas_call | solution.py:439

commit v7 on v6

--- a/solution.py
+++ b/solution.py
@@ -16,7 +16,7 @@
     key=lambda o: -(min(o[0], SIDE - o[0]) + min(o[1], SIDE - o[1])),
 )
 COLUMN_ORDER = (2, 1, 3, 0)
-PIECES = ((0, 256), (256, 512), (512, 768), (768, 896))
+PIECES = ((0, 384), (384, 768), (768, 896))
 
 
 def make_kernel(req, heads, latent, value, rotary, width, hidden, positions):

time: 29 us -> 29.6 us (1.021)
  Pallas kernels: 28.2 us -> 28.9 us
    pallas_call x1, Pallas kernels: 27.6 us -> 28.2 us  [per_device(): pl.pallas_call(make_kernel(req, heads, latent, value, rotary, width, hidd...]
where the time goes in v7:
time: 29.6 us; the launch traced here: 29.5 us
  Pallas kernels  28.9 us (98%)
  between operations  0.64 us (2%)
    pallas_call x1, Pallas kernels, per_device(): pl.pallas_call(make_kernel(req, heads, latent, value, rotary, width, hidd...  28.2 us
    pallas_call x1, Pallas kernels, per_device(): pl.pallas_call(write_out, out_shape=outs, in_specs=[vmem, vmem], out_spec...  0.65 us

profile of v7, /device:TPU:1, one launch (start us, length us, event | category | flops | bytes accessed | tf_op | source)
XLA Modules:
  0.0 29.5 jit_solution(14513509342640800990)
XLA Ops:
  0.6 28.2 %shard_map.104 = (bf16[2,7168]{1,0:T(2,128)(2,1)S(1)}, bf16[64,288]{1,0:T(8,128)(2,1)S(1)}) custom-call(s32[2]{0:T(128)} %lengths_hbm.1, bf16[2,7168]{1,0:T(2,128)(2,1)} %hid_hbm.1, bf16[2,32,576]{2,1,0:T(8,128)(2,1)} %q_hbm.1, bf16[2,224,576]{2,1,0:T(8,128)(2,1)} %cache_hbm.1, bf16[1,512,128]{2,1,0:T(8,128)(2,1)} %wuv_hbm.1, bf16[128,7168]{1,0:T(8,128)(2,1)} %wout_hbm.1, ...), custom_call_target="tpu_custom_call" | custom-call | tf_op jit(solution)/shard_map/pallas_call | solution.py:383
  28.9 0.6 %shard_map.105 = (bf16[2,7168]{1,0:T(2,128)(2,1)}, bf16[64,288]{1,0:T(8,128)(2,1)}) custom-call(bf16[2,7168]{1,0:T(2,128)(2,1)S(1)} %get-tuple-element.4.att_ref, bf16[64,288]{1,0:T(8,128)(2,1)S(1)} %get-tuple-element.5.mlp_ref), custom_call_target="tpu_custom_call" | custom-call | tf_op jit(solution)/shard_map/pallas_call | solution.py:439
